TPU v7x, 32 devices: a whole 2x2x4 slice. The times are simulated.
32 devices in a mesh: groups: 2 (over x), seq: 16 (over z, y, core).
Axes of the slice: x: 2, y: 2, z: 4, core: 2. Of those that a mesh axis runs over, the one named last changes fastest.
Arguments:
- tokens: bfloat16 [1024, 512, 512], P(('groups', 'seq')), parts along dimension 0, may hold values from -6 to 6
- cotangent: bfloat16 [1024, 512, 512], P('groups', 'seq'), parts along dimension 0, may hold values from -6 to 6
- w_first: bfloat16 [512, 512], P('seq'), may hold values from -0.25 to 0.25
- w_second: bfloat16 [512, 512], P('seq'), may hold values from -0.25 to 0.25
- mask_first: int32 [4, 4], replicated, may hold values from 0 to 1, as said below
- mask_second: int32 [4, 4], replicated, may hold values from 0 to 1, as said below
- gate_values: bfloat16 [1024, 512], P(('groups', 'seq')), parts along dimension 0, may hold values from -4 to 4
Outputs:
- grad_tokens: bfloat16 [1024, 512, 512], P(('groups', 'seq')), parts along dimension 0
- grad_first: float32 [1024, 512], P(('groups', 'seq')), parts along dimension 0
- grad_second: float32 [1024, 512], P(('groups', 'seq')), parts along dimension 0
There are 2 independent parts, one for each index of `groups`. A program takes and returns all parts, laid end to end along the dimension named above; an argument that names none is the same for every part. Nothing has to cross between parts.
Inputs may be any that keep to these rules, and one draw needn't show every extreme that they name: `mask_first`: the diagonal blocks of each factor are always kept. `mask_second`: the diagonal blocks of each factor are always kept.
All inputs are finite; a program needn't handle non-finite values.
Results may differ from a plain program's by a relative error of at most 0.0054.
Values may be sent and summed in bfloat16 or wider, within the bound.
A program may use at most 320 MiB of HBM per device.

v0:
```python
import math
import jax
import jax.numpy as jnp
from jax import lax
from jax.sharding import PartitionSpec as P

BLK = 128


def expand_rows(mask, row_ids, extent):
    labels = jnp.arange(mask.shape[0], dtype=jnp.int32)
    row_pick = ((row_ids // BLK)[:, None] == labels[None, :]).astype(jnp.float32)
    col_pick = ((jnp.arange(extent, dtype=jnp.int32) // BLK)[:, None] == labels[None, :]).astype(
        jnp.float32
    )
    return jnp.dot(jnp.dot(row_pick, mask.astype(jnp.float32)), col_pick.T)


def per_device(tokens, cotangent, w_first, w_second, mask_first, mask_second, gate_values):
    position = lax.axis_index("seq")
    extent = tokens.shape[1]
    channels = tokens.shape[2]
    shard_rows = w_first.shape[0]
    row_ids = position * shard_rows + jnp.arange(shard_rows, dtype=jnp.int32)
    keep_first = expand_rows(mask_first, row_ids, extent)
    keep_second = expand_rows(mask_second, row_ids, extent)
    local_first = (w_first.astype(jnp.float32) * keep_first).astype(jnp.bfloat16)
    local_second = (w_second.astype(jnp.float32) * keep_second).astype(jnp.bfloat16)
    full = lax.all_gather(jnp.stack([local_first, local_second]), "seq", axis=1, tiled=True)
    full_first, full_second = (full[0], full[1])
    shards = extent // shard_rows
    flat_cot = cotangent.reshape(extent, -1)
    back_flat = lax.dot_general(
        full_second, flat_cot, (((0,), (0,)), ((), ())), preferred_element_type=jnp.float32
    )
    back_col = back_flat.astype(jnp.bfloat16).reshape(cotangent.shape)
    back_rows = lax.all_to_all(back_col, "seq", split_axis=0, concat_axis=1, tiled=True)
    tokens_late, back_col = lax.optimization_barrier((tokens, back_col))
    gate_full = gate_values.astype(jnp.float32)[:, :, None]
    gated = tokens_late.astype(jnp.float32) * gate_full
    hidden = jnp.einsum("ijc,kj->ikc", tokens_late, full_first, preferred_element_type=jnp.float32)
    mixed = (hidden * gated).astype(jnp.bfloat16)
    mixed, back_rows = lax.optimization_barrier((mixed, back_rows))
    columns = lax.all_to_all(mixed, "seq", split_axis=1, concat_axis=0, tiled=True)
    flat_cols = columns.reshape(extent, -1)
    back_float = back_rows.astype(jnp.float32)
    back_hidden = (back_float * gated).astype(jnp.bfloat16)
    direct = gate_full * back_float * hidden
    through = jnp.einsum("ikc,kj->ijc", back_hidden, full_first, preferred_element_type=jnp.float32)
    grad_tokens = (direct + through).astype(jnp.bfloat16)
    summed_first = lax.psum_scatter(
        jnp.einsum("ikc,ijc->kj", back_hidden, tokens_late, preferred_element_type=jnp.float32),
        "seq",
        scatter_dimension=0,
        tiled=True,
    )
    part_second = lax.dot_general(
        flat_cot, flat_cols, (((1,), (1,)), ((), ())), preferred_element_type=jnp.float32
    )
    spread = lax.all_to_all(
        part_second.reshape(shards, shard_rows, extent),
        "seq",
        split_axis=0,
        concat_axis=0,
        tiled=True,
    )
    summed_second = jnp.sum(spread, axis=0)
    factor = 1.0 / math.sqrt(extent * channels)
    grad_first = keep_first * summed_first * factor
    grad_second = keep_second * summed_second * factor
    return (grad_tokens, grad_first, grad_second)


def solution(mesh):
    in_specs = (
        P(("groups", "seq"), None, None),
        P("groups", "seq", None),
        P("seq", None),
        P("seq", None),
        P(),
        P(),
        P(("groups", "seq"), None),
    )
    out_specs = (
        P(("groups", "seq"), None, None),
        P(("groups", "seq"), None),
        P(("groups", "seq"), None),
    )
    return jax.shard_map(
        per_device, mesh=mesh, in_specs=in_specs, out_specs=out_specs, check_vma=False
    )
```

profile of v0, /device:TPU:0, one launch (start us, length us, event | category | flops | bytes accessed | tf_op | source)
XLA Modules:
  0.0 964.3 jit_solution(4726643977585891241)
XLA Ops:
  7.2 1.1 fusion.14
  8.3 1.1 fusion.17
  9.4 0.8 fusion.23
  10.2 0.6 pad_maximum_fusion
  10.9 18.5 %copy.21 = bf16[64,8,32,512]{3,1,2,0:T(8,128)(2,1)} copy(bf16[64,8,32,512]{3,2,1,0:T(8,128)(2,1)} %bitcast.58) | data formatting | bytes 33554432
  29.3 22.4 %all-gather.2.cloned.1.call-done = bf16[2,512,512]{2,1,0:T(8,128)(2,1)} async-done(((bf16[2,32,512]{2,1,0:T(8,128)(2,1)}), bf16[2,512,512]{2,1,0:T(8,128)(2,1)}) %all-gather.2.cloned.1.call-update) | async-done | bytes 1048592 | tf_op jit(solution)/shard_map/all_gather | solution.py:29
  51.7 15.8 %convolution_convert_fusion = bf16[512,16384]{1,0:T(8,128)(2,1)} fusion(bf16[512,16384]{1,0:T(8,128)(2,1)} %bitcast.53, bf16[2,512,512]{2,1,0:T(8,128)(2,1)} %all-gather.2.cloned.1.call-done), kind=kOutput, calls=%fused_computation.9 | convolution fusion | flops 8598323200 | bytes 34078720 | tf_op jit(solution)/shard_map/dot_general | solution.py:33
  67.5 16.6 %copy.22 = bf16[64,8,32,512]{3,2,1,0:T(8,128)(2,1)} copy(bf16[64,8,32,512]{3,1,2,0:T(8,128)(2,1)} %bitcast.55) | data formatting | bytes 33554432
  84.0 5.5 all-to-all-start
  89.6 28.2 %fusion.4 = (bf16[32,512,512]{2,1,0:T(8,128)(2,1)}, f32[512,32,512]{2,0,1:T(8,128)}) fusion(bf16[32,512,512]{2,1,0:T(8,128)(2,1)} %param.7, f32[32,512]{1,0:T(8,128)S(1)} %convert_element_type.43, bf16[2,512,512]{2,1,0:T(8,128)(2,1)S(1)} %copy-done.1), kind=kOutput, calls=%fused_computation.7 | convolution fusion | flops 8623489024 | bytes 84475904 | tf_op jit(solution)/shard_map/ijc,kj->ikc/dot_general | solution.py:41
  117.7 268.3 %all-to-all-done = bf16[512,32,512]{2,1,0:T(8,128)(2,1)} async-done(((bf16[512,32,512]{2,1,0:T(8,128)(2,1)}), bf16[512,32,512]{2,1,0:T(8,128)(2,1)}, u32[]{:S(2)}, u32[]{:S(2)}) %all-to-all-start) | async-done | bytes 16777248 | tf_op jit(solution)/shard_map/all_to_all | solution.py:37
  386.0 15.1 %copy.15 = bf16[16,32,32,512]{3,2,0,1:T(8,128)(2,1)} copy(bf16[16,32,32,512]{3,2,1,0:T(8,128)(2,1)} %bitcast.6) | data formatting | bytes 33554432 | tf_op jit(solution)/shard_map/all_to_all | solution.py:37
  401.1 1.8 copy-done
  402.9 26.5 %copy.17 = bf16[32,512,512]{2,0,1:T(8,128)(2,1)} copy(bf16[32,512,512]{2,1,0:T(8,128)(2,1)S(1)} %copy-done) | data formatting | bytes 33554432 | tf_op jit(solution)/shard_map/optimization_barrier | solution.py:43
  429.4 70.2 %all-to-all-start.1 = ((bf16[32,512,512]{2,0,1:T(8,128)(2,1)}), bf16[32,512,512]{2,0,1:T(8,128)(2,1)}, u32[]{:S(2)}, u32[]{:S(2)}) async-start(bf16[32,512,512]{2,0,1:T(8,128)(2,1)} %copy.17), calls=%async_computation.2 | async-start | bytes 33554432 | tf_op jit(solution)/shard_map/all_to_all | solution.py:44
  499.9 24.1 %fusion.11 = f32[512,512]{1,0:T(8,128)} fusion(bf16[32,512,512]{2,1,0:T(8,128)(2,1)} %param.7, bf16[32,512,512]{2,1,0:T(8,128)(2,1)} %bitcast.59, f32[32,512]{1,0:T(8,128)S(1)} %convert_element_type.43), kind=kOutput, calls=%fused_computation.12 | convolution fusion | flops 8631877632 | bytes 34668544 | tf_op jit(solution)/shard_map/ikc,ijc->kj/dot_general | solution.py:52
  524.1 278.7 %all-to-all-done.1 = bf16[32,512,512]{2,0,1:T(8,128)(2,1)} async-done(((bf16[32,512,512]{2,0,1:T(8,128)(2,1)}), bf16[32,512,512]{2,0,1:T(8,128)(2,1)}, u32[]{:S(2)}, u32[]{:S(2)}) %all-to-all-start.1) | async-done | bytes 16777248 | tf_op jit(solution)/shard_map/all_to_all | solution.py:44
  802.8 15.8 %copy.18 = bf16[32,16,32,512]{3,2,0,1:T(8,128)(2,1)S(1)} copy(bf16[32,16,32,512]{3,0,2,1:T(8,128)(2,1)} %bitcast.12) | data formatting | bytes 33554432 | tf_op jit(solution)/shard_map/all_to_all | solution.py:44
  818.6 12.2 %copy.23 = bf16[64,8,32,512]{3,1,2,0:T(8,128)(2,1)} copy(bf16[64,8,32,512]{3,2,1,0:T(8,128)(2,1)S(1)} %bitcast.57) | data formatting | bytes 33554432
  830.8 18.0 %fusion.36 = f32[512,512]{0,1:T(8,128)} fusion(bf16[512,16384]{1,0:T(8,128)(2,1)} %bitcast.61, bf16[512,16384]{1,0:T(8,128)(2,1)} %bitcast.54), kind=kOutput, calls=%fused_computation.46 | convolution fusion | flops 8589934592 | bytes 34603008 | tf_op jit(solution)/shard_map/dot_general | solution.py:57
  848.9 70.2 %all-to-all-start.2 = ((f32[16,32,512]{2,1,0:T(8,128)}), f32[16,32,512]{2,1,0:T(8,128)S(1)}, u32[]{:S(2)}, u32[]{:S(2)}) async-start(f32[16,32,512]{2,1,0:T(8,128)} %bitcast.15), calls=%async_computation.3 | async-start | bytes 2097152 | tf_op jit(solution)/shard_map/all_to_all | solution.py:60
  919.1 36.2 %fusion.2 = bf16[32,512,512]{2,1,0:T(8,128)(2,1)} fusion(bf16[32,512,512]{2,1,0:T(8,128)(2,1)} %bitcast.60, f32[512,32,512]{2,0,1:T(8,128)} %get-tuple-element.10, f32[32,512]{1,0:T(8,128)S(1)} %convert_element_type.43, bf16[32,512,512]{2,1,0:T(8,128)(2,1)} %param.7, bf16[2,512,512]{2,1,0:T(8,128)(2,1)S(1)} %copy-done.1), kind=kOutput, calls=%fused_computation.4 | convolution fusion | flops 8673820672 | bytes 101318656 | tf_op jit(solution)/shard_map/ikc,kj->ijc/dot_general | solution.py:49
  955.3 1.5 multiply_multiply_fusion.1
  956.9 0.6 multiply_multiply_fusion
  (23 shorter events, 0.5 us)
Async XLA Ops:
  7.2 44.5 %all-gather.2.cloned.1.call-start = ((), (), s32[]{:S(2)}) async-start(), calls=%async_computation.4 | async-start | bytes 1114112 | tf_op jit(solution)/shard_map/all_gather | solution.py:29
  8.3 21.0 %copy-start.2 = (f32[32,512]{1,0:T(8,128)}, f32[32,512]{1,0:T(8,128)S(1)}, u32[]{:S(2)}) copy-start(f32[32,512]{1,0:T(8,128)S(1)} %fusion.14) | copy-start | bytes 196612
  9.4 19.9 %copy-start.4 = (f32[32,512]{1,0:T(8,128)}, f32[32,512]{1,0:T(8,128)S(1)}, u32[]{:S(2)}) copy-start(f32[32,512]{1,0:T(8,128)S(1)} %fusion.17) | copy-start | bytes 196612
  84.0 5.5 copy-start.6
  84.0 5.5 copy-start.1
  84.0 302.0 %all-to-all-start = ((bf16[512,32,512]{2,1,0:T(8,128)(2,1)}), bf16[512,32,512]{2,1,0:T(8,128)(2,1)}, u32[]{:S(2)}, u32[]{:S(2)}) async-start(bf16[512,32,512]{2,1,0:T(8,128)(2,1)} %bitcast.56), calls=%async_computation | async-start | bytes 33554432 | tf_op jit(solution)/shard_map/all_to_all | solution.py:37
  386.0 16.9 %copy-start = (bf16[32,512,512]{2,1,0:T(8,128)(2,1)S(1)}, bf16[32,512,512]{2,1,0:T(8,128)(2,1)}, u32[]{:S(2)}) copy-start(bf16[32,512,512]{2,1,0:T(8,128)(2,1)} %get-tuple-element.8) | copy-start | bytes 50331652
  429.4 373.4 %all-to-all-start.1 = ((bf16[32,512,512]{2,0,1:T(8,128)(2,1)}), bf16[32,512,512]{2,0,1:T(8,128)(2,1)}, u32[]{:S(2)}, u32[]{:S(2)}) async-start(bf16[32,512,512]{2,0,1:T(8,128)(2,1)} %copy.17), calls=%async_computation.2 | async-start | bytes 33554432 | tf_op jit(solution)/shard_map/all_to_all | solution.py:44
  499.7 455.6 %reduce-scatter.2.cloned.1.call-start = ((), (), s32[]{:S(2)}) async-start(), calls=%async_computation.5 | async-start | bytes 1114112 | tf_op jit(solution)/shard_map/reduce_scatter | solution.py:51
  848.9 107.9 %all-to-all-start.2 = ((f32[16,32,512]{2,1,0:T(8,128)}), f32[16,32,512]{2,1,0:T(8,128)S(1)}, u32[]{:S(2)}, u32[]{:S(2)}) async-start(f32[16,32,512]{2,1,0:T(8,128)} %bitcast.15), calls=%async_computation.3 | async-start | bytes 2097152 | tf_op jit(solution)/shard_map/all_to_all | solution.py:60
  919.1 36.2 %copy-start.5 = (f32[32,512]{1,0:T(8,128)S(1)}, f32[32,512]{1,0:T(8,128)}, u32[]{:S(2)}) copy-start(f32[32,512]{1,0:T(8,128)} %copy-done.4) | copy-start | bytes 196612
  919.1 37.7 %copy-start.3 = (f32[32,512]{1,0:T(8,128)S(1)}, f32[32,512]{1,0:T(8,128)}, u32[]{:S(2)}) copy-start(f32[32,512]{1,0:T(8,128)} %copy-done.2) | copy-start | bytes 196612
Sparse Core Ops, SparseCore 0:
  11.0 40.6 all-gather.1
  524.2 257.9 reduce-scatter.1
where the time goes:
time: 965 us; the launch traced here: 964 us
  waiting for transfers between devices  569 us (59%)
  starting transfers between devices  146 us (15%)
  matrix products  124 us (13%)
  local copies, waits for them, and re-layouts  106 us (11%)
  between operations  14.2 us (1%)
    all_to_all x1, waiting for transfers between devices, per_device(): lax.all_to_all(mixed, 'seq', split_axis=1, concat_axis=0, tiled=True)  279 us
    all_to_all x1, waiting for transfers between devices, per_device(): lax.all_to_all(back_col, 'seq', split_axis=0, concat_axis=1, tiled=True)  268 us
    all_to_all x1, starting transfers between devices, per_device(): lax.all_to_all(part_second.reshape(shards, shard_rows, extent), 'seq', sp...  70.2 us
    all_to_all x1, starting transfers between devices, per_device(): lax.all_to_all(mixed, 'seq', split_axis=1, concat_axis=0, tiled=True)  70.2 us
    unnamed x17, local copies, waits for them, and re-layouts  49 us
    dot_general x1, matrix products, per_device(): jnp.einsum('ikc,kj->ijc', back_hidden, full_first, preferred_element_type...  36.2 us
    dot_general x1, matrix products, per_device(): jnp.einsum('ijc,kj->ikc', tokens_late, full_first, preferred_element_type...  28.2 us
    optimization_barrier x1, local copies, waits for them, and re-layouts, per_device(): mixed, back_rows = lax.optimization_barrier((mixed, back_rows))  26.5 us
  transfers between devices with their start and end apart: 5, of which 3 were waited for; matrix products, arithmetic and copies ran while one was open for 16% of the time, Pallas kernels for 0%

commit v1 on v0

--- a/solution.py
+++ b/solution.py
@@ -5,6 +5,12 @@
 from jax.sharding import PartitionSpec as P
 
 BLK = 128
+
+
+def swap_blocks(block, mesh_axis, split, join):
+    pieces = jnp.split(block, lax.axis_size(mesh_axis), axis=split)
+    incoming = lax.all_to_all(jnp.stack(pieces), mesh_axis, 0, 0)
+    return jnp.concatenate(incoming, axis=join)
 
 
 def expand_rows(mask, row_ids, extent):
@@ -41,7 +47,7 @@
     hidden = jnp.einsum("ijc,kj->ikc", tokens_late, full_first, preferred_element_type=jnp.float32)
     mixed = (hidden * gated).astype(jnp.bfloat16)
     mixed, back_rows = lax.optimization_barrier((mixed, back_rows))
-    columns = lax.all_to_all(mixed, "seq", split_axis=1, concat_axis=0, tiled=True)
+    columns = swap_blocks(mixed, "seq", 1, 0)
     flat_cols = columns.reshape(extent, -1)
     back_float = back_rows.astype(jnp.float32)
     back_hidden = (back_float * gated).astype(jnp.bfloat16)

time: 965 us -> 947 us (0.981)
  local copies, waits for them, and re-layouts: 106 us -> 88.1 us
    optimization_barrier x1 -> x0, local copies, waits for them, and re-layouts: 26.5 us -> none  [per_device(): mixed, back_rows = lax.optimization_barrier((mixed, back_rows))]
    unnamed x17 -> x32, local copies, waits for them, and re-layouts: 49 us -> 72 us
    all_to_all x1 -> x0, local copies, waits for them, and re-layouts: 15.8 us -> none  [per_device(): lax.all_to_all(mixed, 'seq', split_axis=1, concat_axis=0, tiled=True)]
  transfers between devices with their start and end apart: 5 -> 5, of which waited for: 3 -> 3; matrix products, arithmetic and copies ran while one was open for 16% -> 15% of each run, Pallas kernels for 0% -> 0%
where the time goes in v1:
time: 947 us; the launch traced here: 946 us
  waiting for transfers between devices  570 us (60%)
  starting transfers between devices  146 us (15%)
  matrix products  124 us (13%)
  local copies, waits for them, and re-layouts  88.1 us (9%)
  between operations  14.2 us (1%)
    all_to_all x1, waiting for transfers between devices, swap_blocks(): incoming = lax.all_to_all(jnp.stack(pieces), mesh_axis, 0, 0)  279 us
    all_to_all x1, waiting for transfers between devices, per_device(): lax.all_to_all(back_col, 'seq', split_axis=0, concat_axis=1, tiled=True)  268 us
    unnamed x32, local copies, waits for them, and re-layouts  72 us
    all_to_all x1, starting transfers between devices, per_device(): lax.all_to_all(part_second.reshape(shards, shard_rows, extent), 'seq', sp...  70.2 us
    all_to_all x1, starting transfers between devices, swap_blocks(): incoming = lax.all_to_all(jnp.stack(pieces), mesh_axis, 0, 0)  70.2 us
    dot_general x1, matrix products, per_device(): jnp.einsum('ikc,kj->ijc', back_hidden, full_first, preferred_element_type...  36.2 us
    dot_general x1, matrix products, per_device(): jnp.einsum('ijc,kj->ikc', tokens_late, full_first, preferred_element_type...  28.2 us
    dot_general x1, matrix products, per_device(): jnp.einsum('ikc,ijc->kj', back_hidden, tokens_late, preferred_element_typ...  24.1 us
  transfers between devices with their start and end apart: 5, of which 3 were waited for; matrix products, arithmetic and copies ran while one was open for 15% of the time, Pallas kernels for 0%

profile of v1, /device:TPU:0, one launch (start us, length us, event | category | flops | bytes accessed | tf_op | source)
XLA Modules:
  0.0 945.8 jit_solution(4492926866911777404)
XLA Ops:
  10.7 18.5 %copy.14 = bf16[64,8,32,512]{3,1,2,0:T(8,128)(2,1)} copy(bf16[64,8,32,512]{3,2,1,0:T(8,128)(2,1)} %bitcast.87) | data formatting | bytes 33554432
  29.2 22.4 %all-gather.2.cloned.1.call-done = bf16[2,512,512]{2,1,0:T(8,128)(2,1)} async-done(((bf16[2,32,512]{2,1,0:T(8,128)(2,1)}), bf16[2,512,512]{2,1,0:T(8,128)(2,1)}) %all-gather.2.cloned.1.call-update) | async-done | bytes 1048592 | tf_op jit(solution)/shard_map/all_gather | solution.py:35
  51.5 15.8 %convolution_convert_fusion = bf16[512,16384]{1,0:T(8,128)(2,1)} fusion(bf16[512,16384]{1,0:T(8,128)(2,1)} %bitcast.83, bf16[2,512,512]{2,1,0:T(8,128)(2,1)} %all-gather.2.cloned.1.call-done), kind=kOutput, calls=%fused_computation.9 | convolution fusion | flops 8598323200 | bytes 34078720 | tf_op jit(solution)/shard_map/dot_general | solution.py:39
  67.3 16.6 %copy.15 = bf16[64,8,32,512]{3,2,1,0:T(8,128)(2,1)} copy(bf16[64,8,32,512]{3,1,2,0:T(8,128)(2,1)} %bitcast.85) | data formatting | bytes 33554432
  83.9 5.5 all-to-all-start
  89.4 28.2 %fusion.4 = (bf16[32,512,512]{2,1,0:T(8,128)(2,1)}, f32[512,32,512]{2,0,1:T(8,128)}) fusion(bf16[32,512,512]{2,1,0:T(8,128)(2,1)} %param.7, f32[32,512]{1,0:T(8,128)S(1)} %convert_element_type.43, bf16[2,512,512]{2,1,0:T(8,128)(2,1)S(1)} %copy-done.1), kind=kOutput, calls=%fused_computation.7 | convolution fusion | flops 8623489024 | bytes 84475904 | tf_op jit(solution)/shard_map/ijc,kj->ikc/dot_general | solution.py:47
  117.6 268.3 %all-to-all-done = bf16[512,32,512]{2,1,0:T(8,128)(2,1)} async-done(((bf16[512,32,512]{2,1,0:T(8,128)(2,1)}), bf16[512,32,512]{2,1,0:T(8,128)(2,1)}, u32[]{:S(2)}, u32[]{:S(2)}) %all-to-all-start) | async-done | bytes 16777248 | tf_op jit(solution)/shard_map/all_to_all | solution.py:43
  385.9 15.1 %copy.10 = bf16[16,32,32,512]{3,2,0,1:T(8,128)(2,1)} copy(bf16[16,32,32,512]{3,2,1,0:T(8,128)(2,1)} %bitcast.6) | data formatting | bytes 33554432 | tf_op jit(solution)/shard_map/all_to_all | solution.py:43
  400.9 1.8 copy-done
  403.8 1.1 bitcast_dynamic-update-slice_fusion.14
  404.9 1.1 bitcast_dynamic-update-slice_fusion.13
  406.1 1.1 bitcast_dynamic-update-slice_fusion.12
  410.5 1.1 bitcast_dynamic-update-slice_fusion.8
  411.6 1.2 bitcast_dynamic-update-slice_fusion.7
  414.9 1.1 bitcast_dynamic-update-slice_fusion.4
  416.1 1.2 bitcast_dynamic-update-slice_fusion.3
  420.5 70.2 %all-to-all-start.1 = ((bf16[16,32,32,512]{3,2,1,0:T(8,128)(2,1)}), bf16[16,32,32,512]{3,2,1,0:T(8,128)(2,1)}, u32[]{:S(2)}, u32[]{:S(2)}) async-start(bf16[16,32,32,512]{3,2,1,0:T(8,128)(2,1)} %bitcast_dynamic-update-slice_fusion), calls=%async_computation.2 | async-start | bytes 33554432 | tf_op jit(solution)/shard_map/all_to_all | solution.py:12
  490.8 24.1 %fusion.11 = f32[512,512]{1,0:T(8,128)} fusion(bf16[32,512,512]{2,1,0:T(8,128)(2,1)} %param.7, bf16[32,512,512]{2,1,0:T(8,128)(2,1)} %bitcast.88, f32[32,512]{1,0:T(8,128)S(1)} %convert_element_type.43), kind=kOutput, calls=%fused_computation.12 | convolution fusion | flops 8631877632 | bytes 34668544 | tf_op jit(solution)/shard_map/ikc,ijc->kj/dot_general | solution.py:58
  514.9 279.0 %all-to-all-done.1 = bf16[16,32,32,512]{3,2,1,0:T(8,128)(2,1)} async-done(((bf16[16,32,32,512]{3,2,1,0:T(8,128)(2,1)}), bf16[16,32,32,512]{3,2,1,0:T(8,128)(2,1)}, u32[]{:S(2)}, u32[]{:S(2)}) %all-to-all-start.1) | async-done | bytes 16777248 | tf_op jit(solution)/shard_map/all_to_all | solution.py:12
  793.9 18.4 %copy.16 = bf16[64,8,32,512]{3,1,2,0:T(8,128)(2,1)} copy(bf16[64,8,32,512]{3,2,1,0:T(8,128)(2,1)} %bitcast.38) | data formatting | bytes 33554432
  812.3 18.0 %fusion.36 = f32[512,512]{0,1:T(8,128)} fusion(bf16[512,16384]{1,0:T(8,128)(2,1)} %bitcast.90, bf16[512,16384]{1,0:T(8,128)(2,1)} %bitcast.84), kind=kOutput, calls=%fused_computation.62 | convolution fusion | flops 8589934592 | bytes 34603008 | tf_op jit(solution)/shard_map/dot_general | solution.py:63
  830.3 70.2 %all-to-all-start.2 = ((f32[16,32,512]{2,1,0:T(8,128)}), f32[16,32,512]{2,1,0:T(8,128)S(1)}, u32[]{:S(2)}, u32[]{:S(2)}) async-start(f32[16,32,512]{2,1,0:T(8,128)} %bitcast.29), calls=%async_computation.3 | async-start | bytes 2097152 | tf_op jit(solution)/shard_map/all_to_all | solution.py:66
  900.6 36.2 %fusion.2 = bf16[32,512,512]{2,1,0:T(8,128)(2,1)} fusion(bf16[32,512,512]{2,1,0:T(8,128)(2,1)} %bitcast.89, f32[512,32,512]{2,0,1:T(8,128)} %get-tuple-element.10, f32[32,512]{1,0:T(8,128)S(1)} %convert_element_type.43, bf16[32,512,512]{2,1,0:T(8,128)(2,1)} %param.7, bf16[2,512,512]{2,1,0:T(8,128)(2,1)S(1)} %copy-done.1), kind=kOutput, calls=%fused_computation.4 | convolution fusion | flops 8673820672 | bytes 101318656 | tf_op jit(solution)/shard_map/ikc,kj->ijc/dot_general | solution.py:55
  936.8 1.5 multiply_multiply_fusion.1
  (37 shorter events, 14.1 us)
Async XLA Ops:
  7.2 44.4 %all-gather.2.cloned.1.call-start = ((), (), s32[]{:S(2)}) async-start(), calls=%async_computation.4 | async-start | bytes 1114112 | tf_op jit(solution)/shard_map/all_gather | solution.py:35
  8.2 20.9 %copy-start.2 = (f32[32,512]{1,0:T(8,128)}, f32[32,512]{1,0:T(8,128)S(1)}, u32[]{:S(2)}) copy-start(f32[32,512]{1,0:T(8,128)S(1)} %fusion.14) | copy-start | bytes 196612
  9.2 19.9 %copy-start.4 = (f32[32,512]{1,0:T(8,128)}, f32[32,512]{1,0:T(8,128)S(1)}, u32[]{:S(2)}) copy-start(f32[32,512]{1,0:T(8,128)S(1)} %fusion.17) | copy-start | bytes 196612
  83.9 5.5 copy-start.6
  83.9 5.5 copy-start.1
  83.9 302.0 %all-to-all-start = ((bf16[512,32,512]{2,1,0:T(8,128)(2,1)}), bf16[512,32,512]{2,1,0:T(8,128)(2,1)}, u32[]{:S(2)}, u32[]{:S(2)}) async-start(bf16[512,32,512]{2,1,0:T(8,128)(2,1)} %bitcast.86), calls=%async_computation | async-start | bytes 33554432 | tf_op jit(solution)/shard_map/all_to_all | solution.py:43
  385.9 16.9 %copy-start = (bf16[32,512,512]{2,1,0:T(8,128)(2,1)S(1)}, bf16[32,512,512]{2,1,0:T(8,128)(2,1)}, u32[]{:S(2)}) copy-start(bf16[32,512,512]{2,1,0:T(8,128)(2,1)} %get-tuple-element.8) | copy-start | bytes 50331652
  420.5 373.4 %all-to-all-start.1 = ((bf16[16,32,32,512]{3,2,1,0:T(8,128)(2,1)}), bf16[16,32,32,512]{3,2,1,0:T(8,128)(2,1)}, u32[]{:S(2)}, u32[]{:S(2)}) async-start(bf16[16,32,32,512]{3,2,1,0:T(8,128)(2,1)} %bitcast_dynamic-update-slice_fusion), calls=%async_computation.2 | async-start | bytes 33554432 | tf_op jit(solution)/shard_map/all_to_all | solution.py:12
  490.8 446.0 %reduce-scatter.2.cloned.1.call-start = ((), (), s32[]{:S(2)}) async-start(), calls=%async_computation.5 | async-start | bytes 1114112 | tf_op jit(solution)/shard_map/reduce_scatter | solution.py:57
  830.3 107.9 %all-to-all-start.2 = ((f32[16,32,512]{2,1,0:T(8,128)}), f32[16,32,512]{2,1,0:T(8,128)S(1)}, u32[]{:S(2)}, u32[]{:S(2)}) async-start(f32[16,32,512]{2,1,0:T(8,128)} %bitcast.29), calls=%async_computation.3 | async-start | bytes 2097152 | tf_op jit(solution)/shard_map/all_to_all | solution.py:66
  900.6 36.2 %copy-start.5 = (f32[32,512]{1,0:T(8,128)S(1)}, f32[32,512]{1,0:T(8,128)}, u32[]{:S(2)}) copy-start(f32[32,512]{1,0:T(8,128)} %copy-done.4) | copy-start | bytes 196612
  900.6 37.8 %copy-start.3 = (f32[32,512]{1,0:T(8,128)S(1)}, f32[32,512]{1,0:T(8,128)}, u32[]{:S(2)}) copy-start(f32[32,512]{1,0:T(8,128)} %copy-done.2) | copy-start | bytes 196612
Sparse Core Ops, SparseCore 0:
  10.8 40.6 all-gather.1
  515.0 258.1 reduce-scatter.1
